TPU v7x, 256 devices: a whole 4x4x8 slice. The times are simulated.
256 devices in a mesh: img: 64 (over y, z_lo, x, core), slab: 4 (over z_hi).
Axes of the slice: x: 4, y: 4, z: 8 (z_hi: 4, z_lo: 2; z = z_hi * 2 + z_lo), core: 2. Of those that a mesh axis runs over, the one named last changes fastest.
Arguments:
- images: bfloat16 [4096, 32768], P('img'), may hold values from -6 to 6
- references: bfloat16 [2, 128, 32768], P(None, 'slab'), may hold values from -6 to 6
- orientations: int32 [4096, 2, 64], P('img'), may hold values from 0 to 127
- ctf_table: float32 [4096, 64], P('img'), may hold values from -1 to 1
- inv_noise: float32 [4096], P('img'), may hold values from 0.002 to 0.02
- class_weight: float32 [2], replicated, may hold values from 0.2 to 5
Outputs:
- updated_volume: float32 [2, 128, 32768], P(None, 'slab', 'img')
All inputs are finite; a program needn't handle non-finite values.
Results may differ from a plain program's by a relative error of at most 0.0065.
Values sent between devices are 32-bit elements; how exact they have to be, the bound alone decides.
A program may use at most 192 MiB of HBM per device.

v0:
```python
import jax
import jax.numpy as jnp
from jax import lax
from jax.sharding import PartitionSpec as P

BOX = 128
SHELLS = 64


def shell_index():
    position = jnp.arange(BOX * BOX, dtype=jnp.int32)
    column = position % BOX - BOX // 2
    row_place = position // BOX - BOX // 2
    radius_sq = column * column + row_place * row_place
    levels = jnp.arange(1, SHELLS, dtype=jnp.int32)
    inside = (2 * levels[None, :] * levels[None, :] <= radius_sq[:, None]).astype(jnp.int32)
    return jnp.sum(inside, axis=1)


def contract_first(left, right):
    return lax.dot_general(
        left, right, (((0,), (0,)), ((), ())), preferred_element_type=jnp.float32
    )


def contract_last(left, right):
    return lax.dot_general(
        left, right, (((1,), (1,)), ((), ())), preferred_element_type=jnp.float32
    )


def shards(images, references, orientations, ctf_table, inv_noise, class_weight):
    batch = images.shape[0]
    classes, local_planes, width = references.shape
    pixels = width // 2
    levels = jnp.arange(SHELLS, dtype=jnp.int32)
    selector = (shell_index()[None, :] == levels[:, None]).astype(jnp.float32)
    ctf_pixel = jnp.dot(
        ctf_table, selector, precision=lax.Precision.HIGHEST, preferred_element_type=jnp.float32
    )
    weighted = (images.astype(jnp.float32) * jnp.repeat(ctf_pixel, 2, axis=1)).astype(jnp.bfloat16)
    ctf_square = (ctf_pixel * ctf_pixel).astype(jnp.bfloat16)
    planes = references.reshape(classes * local_planes, width)
    spread = references.astype(jnp.float32).reshape(classes * local_planes, pixels, 2)
    power = jnp.sum(spread * spread, axis=2).astype(jnp.bfloat16)
    intersection = contract_last(weighted, planes)
    energy = contract_last(ctf_square, power)
    local_table = (2.0 * intersection - energy).reshape(batch, classes, local_planes)
    offset = lax.axis_index("slab") * local_planes
    relative = orientations - offset
    inside = (relative >= 0) & (relative < local_planes)
    prior = jnp.log(class_weight)[None, :, None]
    table = lax.all_gather(local_table, "slab", axis=2, tiled=True)
    picked = jnp.take_along_axis(table, orientations, axis=2)
    scores = prior + inv_noise[:, None, None] * picked
    peak = jnp.max(scores, axis=(1, 2), keepdims=True)
    expo = jnp.exp(scores - peak)
    resp = expo / jnp.sum(expo, axis=(1, 2), keepdims=True)
    local_resp = jnp.where(inside, resp, 0.0)
    plane_ids = jnp.arange(local_planes, dtype=jnp.int32)
    hits = (relative[:, :, :, None] == plane_ids[None, None, None, :]).astype(jnp.float32)
    per_plane = jnp.einsum("bkl,bklp->bkp", local_resp, hits).astype(jnp.bfloat16)
    flat_plane = per_plane.reshape(batch, classes * local_planes)
    planes_here = classes * local_planes
    share = width // lax.axis_size("img")
    square_pairs = jnp.repeat(ctf_square, 2, axis=1)
    summed = lax.psum_scatter(
        jnp.concatenate(
            [contract_first(weighted, flat_plane), contract_first(square_pairs, flat_plane)], axis=1
        ),
        "img",
        scatter_dimension=0,
        tiled=True,
    )
    numerator = summed[:, :planes_here]
    weight_sum = summed[:, planes_here:]
    updated = numerator / (weight_sum + 1.0)
    return jnp.transpose(updated).reshape(classes, local_planes, share)


def solution(mesh):
    return jax.shard_map(
        shards,
        mesh=mesh,
        in_specs=(
            P("img", None),
            P(None, "slab", None),
            P("img", None, None),
            P("img", None),
            P("img"),
            P(),
        ),
        out_specs=P(None, "slab", "img"),
        check_vma=False,
    )
```

profile of v0, /device:TPU:64, one launch (start us, length us, event | category | flops | bytes accessed | tf_op | source)
XLA Modules:
  0.0 655.7 jit_solution(16767141017079133494)
XLA Ops:
  6.6 0.6 convert_reduce_fusion
  7.2 0.1 copy-done
  7.3 3.9 multiply_convert_fusion.1
  11.2 6.9 %copy.33 = f32[64,16384]{0,1:T(8,128)} copy(f32[64,16384]{1,0:T(8,128)} %get-tuple-element.10) | data formatting | bytes 8388608 | tf_op jit(solution)/shard_map/dot_general | solution.py:38
  18.1 8.4 %copy.32 = bf16[64,32768]{0,1:T(8,128)(2,1)} copy(bf16[64,32768]{1,0:T(8,128)(2,1)} %param.6) | data formatting | bytes 8388608 | tf_op args[0]
  26.5 6.0 convert_multiply_fusion
  32.4 37.3 %copy.34 = f32[2,32,32768]{1,0,2:T(2,128)} copy(f32[2,32,32768]{2,1,0:T(8,128)} %convert_multiply_fusion) | data formatting | bytes 16777216 | tf_op jit(solution)/shard_map/mul | solution.py:45
  69.8 37.1 %mul.74 = f32[64,16384,2]{0,2,1:T(2,128)} reshape(f32[2,32,32768]{1,0,2:T(2,128)} %copy.34) | data formatting | bytes 16777216 | tf_op jit(solution)/shard_map/mul | solution.py:45
  106.9 3.2 copy.37
  110.1 73.2 %reduce_sum.28 = bf16[64,16384]{0,1:T(8,128)(2,1)} reduce(f32[64,16384,2]{0,2,1:T(2,128)} %mul.74, f32[]{:T(128)} %constant.64.clone.1), dimensions={2}, to_apply=%region_1.2 | reduce | flops 1048576 | bytes 10485764 | tf_op jit(solution)/shard_map/reduce_sum | solution.py:45
  183.2 9.6 %broadcast_in_dim.11 = f32[64,16384,2]{0,2,1:T(2,128)} broadcast(f32[64,16384]{0,1:T(8,128)} %copy.33), dimensions={0,1} | broadcast | bytes 12582912 | tf_op jit(solution)/shard_map/broadcast_in_dim | solution.py:41
  192.8 0.3 copy-done.3
  193.2 10.8 %convolution_multiply_fusion = f32[64,64]{1,0:T(8,128)S(1)} fusion(bf16[64,32768]{1,0:T(8,128)(2,1)S(1)} %bitcast.33, f32[64,32768]{0,1:T(8,128)} %bitcast.30, bf16[64,32768]{0,1:T(8,128)(2,1)} %copy.32), kind=kOutput, calls=%fused_computation.14 | convolution fusion | flops 274731008 | bytes 16793600 | tf_op jit(solution)/shard_map/dot_general | solution.py:27
  204.0 3.1 fusion.4
  207.1 0.1 copy.35
  207.2 15.6 %all_gather.3 = f32[64,2,128]{0,1,2:T(2,128)S(1)} all-gather(f32[64,2,32]{0,1,2:T(2,128)S(1)} %copy.36), channel_id=1, replica_groups=mesh['img'=64,'slab'=4] {'slab'}, dimensions={2}, use_global_device_ids=true | all-gather | bytes 81920 | tf_op jit(solution)/shard_map/all_gather | solution.py:53
  222.8 0.1 bitcast_or_fusion
  222.9 0.1 reshape.75
  223.0 74.9 %gather_fusion = f32[8192]{0:T(1024)S(1)} fusion(f32[64,2,128]{0,1,2:T(2,128)S(1)} %all_gather.3, s32[8192]{0:T(1024)S(1)} %reshape.75), kind=kCustom, calls=%fused_computation | custom fusion | bytes 163840 | tf_op jit(solution)/shard_map/jit(take_along_axis)/gather | solution.py:54
  297.9 0.1 reshape.78
  298.0 0.9 fusion.25
  299.0 1.0 fusion.23
  300.0 0.2 and_select_fusion.1
  300.2 0.7 fusion.3
  300.8 0.1 copy.39
  300.9 11.3 %fusion.24 = f32[32768,64]{0,1:T(8,128)S(1)} fusion(bf16[64,64]{0,1:T(8,128)(2,1)S(1)} %bitcast.34, f32[64,32768]{0,1:T(8,128)} %bitcast.31, bf16[64,32768]{0,1:T(8,128)(2,1)} %copy.32), kind=kOutput, calls=%fused_computation.45 | convolution fusion | flops 274726912 | bytes 20979712 | tf_op jit(solution)/shard_map/dot_general | solution.py:21
  312.3 5.6 broadcast_in_dim.15
  317.8 6.4 fusion.27
  324.2 6.1 pad_maximum_fusion
  330.3 0.0 reduce-scatter.2.cloned.1.call-update
  330.4 316.8 %reduce-scatter.2.cloned.1.call-done = f32[512,128]{0,1:T(8,128)} async-done(((f32[32768,128]{0,1:T(8,128)}), f32[512,128]{0,1:T(8,128)}) %reduce-scatter.2.cloned.1.call-update) | async-done | bytes 262160 | tf_op jit(solution)/shard_map/reduce_scatter | solution.py:67
  647.2 1.6 fusion.8
  (17 shorter events, 0.1 us)
Async XLA Ops:
  6.5 0.8 copy-start
  6.5 640.7 %reduce-scatter.2.cloned.1.call-start = ((), (), s32[]{:S(2)}) async-start(), calls=%async_computation.1 | async-start | bytes 17039360 | tf_op jit(solution)/shard_map/reduce_scatter | solution.py:67
  183.2 9.9 %copy-start.3 = (bf16[2,32,32768]{2,1,0:T(8,128)(2,1)S(1)}, bf16[2,32,32768]{2,1,0:T(8,128)(2,1)}, u32[]{:S(2)}) copy-start(bf16[2,32,32768]{2,1,0:T(8,128)(2,1)} %param.7) | copy-start | bytes 12582916
  204.0 18.9 %copy-start.4 = (s32[64,2,64]{2,1,0:T(2,128)S(1)}, s32[64,2,64]{2,1,0:T(2,128)}, u32[]{:S(2)}) copy-start(s32[64,2,64]{2,1,0:T(2,128)} %param.8) | copy-start | bytes 98308
  223.0 75.0 %copy-start.6 = (f32[2]{0:T(128)S(1)}, f32[2]{0:T(128)}, u32[]{:S(2)}) copy-start(f32[2]{0:T(128)} %param.11) | copy-start | bytes 28
  223.0 75.0 %copy-start.5 = (f32[64]{0:T(128)S(1)}, f32[64]{0:T(128)}, u32[]{:S(2)}) copy-start(f32[64]{0:T(128)} %param.10) | copy-start | bytes 772
  300.9 11.3 %copy-start.2 = (bf16[64,16384]{0,1:T(8,128)(2,1)S(1)}, bf16[64,16384]{0,1:T(8,128)(2,1)}, u32[]{:S(2)}) copy-start(bf16[64,16384]{0,1:T(8,128)(2,1)} %copy.37) | copy-start | bytes 6291460
  330.4 318.5 %copy-start.1 = (f32[64,64]{1,0:T(8,128)S(1)}, f32[64,64]{1,0:T(8,128)}, u32[]{:S(2)}) copy-start(f32[64,64]{1,0:T(8,128)} %param.9) | copy-start | bytes 49156
Sparse Core Ops, SparseCore 0:
  330.5 316.6 reduce-scatter.1
where the time goes:
time: 658 us; the launch traced here: 656 us
  waiting for transfers between devices  317 us (48%)
  local copies, waits for them, and re-layouts  184 us (28%)
  other arithmetic  89.7 us (14%)
  matrix products  36.2 us (6%)
  blocking collectives  15.6 us (2%)
  between operations  13.5 us (2%)
    reduce_scatter x1, waiting for transfers between devices, shards(): lax.psum_scatter(jnp.concatenate([contract_first(weighted, flat_plane), c...  317 us
    gather x3, local copies, waits for them, and re-layouts, shards(): picked = jnp.take_along_axis(table, orientations, axis=2)  75.1 us
    mul x2, local copies, waits for them, and re-layouts, shards(): power = jnp.sum(spread * spread, axis=2).astype(jnp.bfloat16)  74.5 us
    reduce_sum x1, other arithmetic, shards(): power = jnp.sum(spread * spread, axis=2).astype(jnp.bfloat16)  73.2 us
    dot_general x2, matrix products, contract_first(): lax.dot_general(left, right, (((0,), (0,)), ((), ())), preferred_element_...  17.7 us
    all_gather x1, blocking collectives, shards(): table = lax.all_gather(local_table, 'slab', axis=2, tiled=True)  15.6 us
    dot_general x2, matrix products, contract_last(): lax.dot_general(left, right, (((1,), (1,)), ((), ())), preferred_element_...  13.9 us
  transfers between devices with their start and end apart: 1, of which 1 were waited for; matrix products, arithmetic and copies ran while one was open for 0% of the time, Pallas kernels for 0%

commit v1 on v0

--- a/solution.py
+++ b/solution.py
@@ -50,7 +50,9 @@
     relative = orientations - offset
     inside = (relative >= 0) & (relative < local_planes)
     prior = jnp.log(class_weight)[None, :, None]
-    table = lax.all_gather(local_table, "slab", axis=2, tiled=True)
+    table = jnp.concatenate(
+        lax.all_to_all(jnp.stack([local_table] * lax.axis_size("slab")), "slab", 0, 0), axis=2
+    )
     picked = jnp.take_along_axis(table, orientations, axis=2)
     scores = prior + inv_noise[:, None, None] * picked
     peak = jnp.max(scores, axis=(1, 2), keepdims=True)

time: 658 us -> 648 us (0.985)
  blocking collectives: 15.6 us -> 0 us
  starting transfers between devices: 0.01 us -> 8.11 us
    all_gather x1 -> x0, blocking collectives: 15.6 us -> none  [shards(): table = lax.all_gather(local_table, 'slab', axis=2, tiled=True)]
    all_to_all x0 -> x1, starting transfers between devices: none -> 8.11 us  [shards(): lax.all_to_all(jnp.stack([local_table] * lax.axis_size('slab')), 'slab',...]
    gather x3, local copies, waits for them, and re-layouts: 75.1 us -> 68.4 us  [shards(): picked = jnp.take_along_axis(table, orientations, axis=2)]
  transfers between devices with their start and end apart: 1 -> 2, of which waited for: 1 -> 2; matrix products, arithmetic and copies ran while one was open for 0% -> 1% of each run, Pallas kernels for 0% -> 0%
where the time goes in v1:
time: 648 us; the launch traced here: 646 us
  waiting for transfers between devices  319 us (49%)
  local copies, waits for them, and re-layouts  179 us (28%)
  other arithmetic  90.5 us (14%)
  matrix products  36.2 us (6%)
  between operations  13.5 us (2%)
  starting transfers between devices  8.11 us (1%)
    reduce_scatter x1, waiting for transfers between devices, shards(): lax.psum_scatter(jnp.concatenate([contract_first(weighted, flat_plane), c...  317 us
    mul x2, local copies, waits for them, and re-layouts, shards(): power = jnp.sum(spread * spread, axis=2).astype(jnp.bfloat16)  74.5 us
    reduce_sum x1, other arithmetic, shards(): power = jnp.sum(spread * spread, axis=2).astype(jnp.bfloat16)  73.1 us
    gather x3, local copies, waits for them, and re-layouts, shards(): picked = jnp.take_along_axis(table, orientations, axis=2)  68.4 us
    dot_general x2, matrix products, contract_first(): lax.dot_general(left, right, (((0,), (0,)), ((), ())), preferred_element_...  17.7 us
    dot_general x2, matrix products, contract_last(): lax.dot_general(left, right, (((1,), (1,)), ((), ())), preferred_element_...  13.9 us
  transfers between devices with their start and end apart: 2, of which 2 were waited for; matrix products, arithmetic and copies ran while one was open for 1% of the time, Pallas kernels for 0%

profile of v1, /device:TPU:64, one launch (start us, length us, event | category | flops | bytes accessed | tf_op | source)
XLA Modules:
  0.0 645.8 jit_solution(16199360637496724657)
XLA Ops:
  6.6 0.6 convert_reduce_fusion
  7.2 0.1 copy-done
  7.3 3.9 multiply_convert_fusion.1
  11.2 6.9 %copy.31 = f32[64,16384]{0,1:T(8,128)} copy(f32[64,16384]{1,0:T(8,128)} %get-tuple-element.10) | data formatting | bytes 8388608 | tf_op jit(solution)/shard_map/dot_general | solution.py:38
  18.1 8.4 %copy.30 = bf16[64,32768]{0,1:T(8,128)(2,1)} copy(bf16[64,32768]{1,0:T(8,128)(2,1)} %param.6) | data formatting | bytes 8388608 | tf_op args[0]
  26.5 6.0 convert_multiply_fusion
  32.4 37.3 %copy.32 = f32[2,32,32768]{1,0,2:T(2,128)} copy(f32[2,32,32768]{2,1,0:T(8,128)} %convert_multiply_fusion) | data formatting | bytes 16777216 | tf_op jit(solution)/shard_map/mul | solution.py:45
  69.8 37.1 %mul.74 = f32[64,16384,2]{0,2,1:T(2,128)} reshape(f32[2,32,32768]{1,0,2:T(2,128)} %copy.32) | data formatting | bytes 16777216 | tf_op jit(solution)/shard_map/mul | solution.py:45
  106.9 73.1 %reduce_sum.28 = bf16[64,16384]{0,1:T(8,128)(2,1)} reduce(f32[64,16384,2]{0,2,1:T(2,128)} %mul.74, f32[]{:T(128)} %constant.64.clone.1), dimensions={2}, to_apply=%region_1.2 | reduce | flops 1048576 | bytes 10485764 | tf_op jit(solution)/shard_map/reduce_sum | solution.py:45
  180.0 9.6 %broadcast_in_dim.11 = f32[64,16384,2]{0,2,1:T(2,128)} broadcast(f32[64,16384]{0,1:T(8,128)} %copy.31), dimensions={0,1} | broadcast | bytes 12582912 | tf_op jit(solution)/shard_map/broadcast_in_dim | solution.py:41
  189.6 0.3 copy-done.3
  189.9 10.8 %convolution_multiply_fusion = f32[64,64]{1,0:T(8,128)S(1)} fusion(bf16[64,32768]{1,0:T(8,128)(2,1)S(1)} %bitcast.41, f32[64,32768]{0,1:T(8,128)} %bitcast.38, bf16[64,32768]{0,1:T(8,128)(2,1)} %copy.30), kind=kOutput, calls=%fused_computation.14 | convolution fusion | flops 274731008 | bytes 16793600 | tf_op jit(solution)/shard_map/dot_general | solution.py:27
  200.8 3.1 fusion.4
  204.0 0.8 reshape.94
  204.7 8.1 %all-to-all-start = ((f32[4,1,4096]{2,1,0:T(1,128)}), f32[4,1,4096]{2,1,0:T(1,128)S(1)}, u32[]{:S(2)}, u32[]{:S(2)}) async-start(f32[4,1,4096]{2,1,0:T(1,128)} %reshape.94), calls=%async_computation | async-start | bytes 131072 | tf_op jit(solution)/shard_map/all_to_all | solution.py:54
  212.9 3.4 copy.35
  216.3 0.1 reshape.81
  216.5 2.2 all-to-all-done
  218.6 0.5 broadcast.117
  219.1 0.8 reduce
  219.9 0.1 reshape.95
  220.1 68.2 %gather_fusion = f32[8192]{0:T(1024)S(1)} fusion(f32[64,2,128]{0,2,1:T(8,128)S(1)} %bitcast.37, s32[8192]{0:T(1024)S(1)} %reshape.81), kind=kCustom, calls=%fused_computation | custom fusion | bytes 163840 | tf_op jit(solution)/shard_map/jit(take_along_axis)/gather | solution.py:56
  288.4 0.9 fusion.25
  289.4 1.0 fusion.23
  290.4 0.2 and_select_fusion.1
  290.6 0.7 fusion.3
  291.3 11.3 %fusion.24 = f32[32768,64]{0,1:T(8,128)S(1)} fusion(bf16[64,64]{0,1:T(8,128)(2,1)S(1)} %bitcast.42, f32[64,32768]{0,1:T(8,128)} %bitcast.39, bf16[64,32768]{0,1:T(8,128)(2,1)} %copy.30), kind=kOutput, calls=%fused_computation.45 | convolution fusion | flops 274726912 | bytes 20979712 | tf_op jit(solution)/shard_map/dot_general | solution.py:21
  302.7 5.6 broadcast_in_dim.15
  308.2 6.4 fusion.27
  314.6 6.1 pad_maximum_fusion
  320.8 316.5 %reduce-scatter.2.cloned.1.call-done = f32[512,128]{0,1:T(8,128)} async-done(((f32[32768,128]{0,1:T(8,128)}), f32[512,128]{0,1:T(8,128)}) %reduce-scatter.2.cloned.1.call-update) | async-done | bytes 262160 | tf_op jit(solution)/shard_map/reduce_scatter | solution.py:69
  637.3 1.6 fusion.8
  (24 shorter events, 0.5 us)
Async XLA Ops:
  6.5 0.8 copy-start
  180.0 9.9 %copy-start.3 = (bf16[2,32,32768]{2,1,0:T(8,128)(2,1)S(1)}, bf16[2,32,32768]{2,1,0:T(8,128)(2,1)}, u32[]{:S(2)}) copy-start(bf16[2,32,32768]{2,1,0:T(8,128)(2,1)} %param.7) | copy-start | bytes 12582916
  200.8 12.1 %copy-start.4 = (s32[64,2,64]{2,1,0:T(2,128)S(1)}, s32[64,2,64]{2,1,0:T(2,128)}, u32[]{:S(2)}) copy-start(s32[64,2,64]{2,1,0:T(2,128)} %param.8) | copy-start | bytes 98308
  203.9 12.6 %copy-start.6 = (f32[2]{0:T(128)S(1)}, f32[2]{0:T(128)}, u32[]{:S(2)}) copy-start(f32[2]{0:T(128)} %param.11) | copy-start | bytes 28
  204.7 13.9 %all-to-all-start = ((f32[4,1,4096]{2,1,0:T(1,128)}), f32[4,1,4096]{2,1,0:T(1,128)S(1)}, u32[]{:S(2)}, u32[]{:S(2)}) async-start(f32[4,1,4096]{2,1,0:T(1,128)} %reshape.94), calls=%async_computation | async-start | bytes 131072 | tf_op jit(solution)/shard_map/all_to_all | solution.py:54
  212.8 424.4 %reduce-scatter.2.cloned.1.call-start = ((), (), s32[]{:S(2)}) async-start(), calls=%async_computation.2 | async-start | bytes 17039360 | tf_op jit(solution)/shard_map/reduce_scatter | solution.py:69
  220.1 68.3 %copy-start.5 = (f32[64]{0:T(128)S(1)}, f32[64]{0:T(128)}, u32[]{:S(2)}) copy-start(f32[64]{0:T(128)} %param.10) | copy-start | bytes 772
  291.3 11.3 %copy-start.2 = (bf16[64,16384]{0,1:T(8,128)(2,1)S(1)}, bf16[64,16384]{0,1:T(8,128)(2,1)}, u32[]{:S(2)}) copy-start(bf16[64,16384]{0,1:T(8,128)(2,1)} %copy.35) | copy-start | bytes 6291460
  320.8 318.2 %copy-start.1 = (f32[64,64]{1,0:T(8,128)S(1)}, f32[64,64]{1,0:T(8,128)}, u32[]{:S(2)}) copy-start(f32[64,64]{1,0:T(8,128)} %param.9) | copy-start | bytes 49156
Sparse Core Ops, SparseCore 0:
  320.9 316.3 reduce-scatter.1
